TPU v7x, 512 devices: a whole 4x4x16 slice. The times are simulated.
512 devices in a mesh: dp: 16 (over y, x), seq: 32 (over z, core).
Axes of the slice: x: 4, y: 4, z: 16, core: 2. Of those that a mesh axis runs over, the one named last changes fastest.
Arguments:
- tokens: bfloat16 [16, 8192, 4096], P('dp', 'seq'), may hold values from -6 to 6
- w_qkv: bfloat16 [4096, 768], P('dp'), may hold values from -0.09375 to 0.09375
- norm_gain: float32 [256], replicated, may hold values from 0.1 to 1.9
- w_out: bfloat16 [256, 4096], P(None, 'dp'), may hold values from -0.375 to 0.375
Outputs:
- mixed: bfloat16 [16, 8192, 4096], P('dp', 'seq')
All inputs are finite; a program needn't handle non-finite values.
Results may differ from a plain program's by a relative error of at most 0.015.
Values may be sent and summed in bfloat16 or wider, within the bound.
A program may use at most 64 MiB of HBM per device.

v0:
```python
import jax
import jax.numpy as jnp
from jax import lax
from jax.sharding import PartitionSpec as P

HEAD = 128


def shards(tokens, w_qkv, norm_gain, w_out):
    inputs = tokens[0]
    tok_rows = inputs.shape[0]
    width3 = w_qkv.shape[1]
    feat = width3 // 3
    heads = norm_gain.shape[0] // HEAD
    proj = jnp.dot(
        inputs, lax.all_gather(w_qkv, "dp", axis=0, tiled=True), preferred_element_type=jnp.float32
    )
    query = jax.nn.silu(proj[:, :feat]).astype(jnp.bfloat16).reshape(tok_rows, heads, HEAD)
    keys = jax.nn.silu(proj[:, feat : 2 * feat]).astype(jnp.bfloat16).reshape(tok_rows, heads, HEAD)
    values = proj[:, 2 * feat :].astype(jnp.bfloat16).reshape(tok_rows, heads, HEAD)
    state = jnp.einsum("thA,thB->hAB", keys, values, preferred_element_type=jnp.float32)
    every_state = lax.all_gather(
        state[None].astype(jnp.bfloat16), "seq", axis=0, tiled=True
    ).astype(jnp.float32)
    blocks = every_state.shape[0]
    weights = (jnp.arange(blocks) < lax.axis_index("seq")).astype(jnp.float32)
    prefix = jnp.einsum("n,nhab->hab", weights, every_state, precision=lax.Precision.HIGHEST)
    prefix = prefix.astype(jnp.bfloat16)
    inter = jnp.einsum("thA,hAB->thB", query, prefix, preferred_element_type=jnp.float32)
    scores = jnp.einsum("thA,shA->hts", query, keys, preferred_element_type=jnp.float32)
    rows = jnp.arange(tok_rows)
    causal = rows[:, None] >= rows[None, :]
    scores = jnp.where(causal[None], scores, 0.0).astype(jnp.bfloat16)
    intra = jnp.einsum("hts,shB->thB", scores, values, preferred_element_type=jnp.float32)
    attended = inter + intra
    meansq = jnp.mean(attended * attended, axis=-1, keepdims=True)
    normed = attended * lax.rsqrt(meansq + 1e-06) * norm_gain.reshape(heads, HEAD)
    normed = normed.astype(jnp.bfloat16).reshape(tok_rows, heads * HEAD)
    mixed = jnp.dot(
        normed, lax.all_gather(w_out, "dp", axis=1, tiled=True), preferred_element_type=jnp.float32
    )
    return mixed.astype(jnp.bfloat16)[None]


def solution(mesh):
    return jax.shard_map(
        shards,
        mesh=mesh,
        in_specs=(P("dp", "seq", None), P("dp", None), P(), P(None, "dp")),
        out_specs=P("dp", "seq", None),
        check_vma=False,
    )
```

profile of v0, /device:TPU:1, one launch (start us, length us, event | category | flops | bytes accessed | tf_op | source)
XLA Modules:
  0.0 242.1 jit_solution(8243178207157146970)
XLA Ops:
  6.5 0.0 copy-start
  6.5 0.0 all-gather.5.cloned.1.call-start
  6.5 0.7 all-gather.5.cloned.1.call-update
  7.3 0.0 all-gather.9.cloned.1.call-start
  7.3 85.1 %all-gather.5.cloned.1.call-done = bf16[4096,768]{1,0:T(8,128)(2,1)} async-done(((bf16[256,768]{1,0:T(8,128)(2,1)}), bf16[4096,768]{1,0:T(8,128)(2,1)}) %all-gather.5.cloned.1.call-update) | async-done | bytes 6291472 | tf_op jit(solution)/shard_map/all_gather | solution.py:16
  92.4 0.0 copy-done
  92.4 4.6 %fusion.1 = f32[256,768]{1,0:T(8,128)S(1)} fusion(bf16[4096,768]{1,0:T(8,128)(2,1)} %all-gather.5.cloned.1.call-done, bf16[1,256,4096]{2,1,0:T(8,128)(2,1)S(1)} %copy-done), kind=kOutput, calls=%fused_computation.2 | convolution fusion | flops 1610612736 | bytes 9175040 | tf_op jit(solution)/shard_map/dot_general | solution.py:15
  96.9 0.1 fusion.13
  97.1 0.1 copy.16
  97.2 0.1 copy.17
  97.3 0.8 convolution_convert_fusion.1
  98.2 0.0 all-gather.9.cloned.1.call-update
  98.2 0.0 copy-start.1
  98.2 0.0 all-gather.7.cloned.1.call-start
  98.2 0.7 all-gather.7.cloned.1.call-update
  99.0 0.4 fusion.6
  99.3 71.0 %all-gather.9.cloned.1.call-done = bf16[64,128,128]{2,1,0:T(8,128)(2,1)} async-done(((bf16[2,128,128]{2,1,0:T(8,128)(2,1)}), bf16[64,128,128]{2,1,0:T(8,128)(2,1)}) %all-gather.9.cloned.1.call-update) | async-done | bytes 2097168 | tf_op jit(solution)/shard_map/all_gather | solution.py:22
  170.3 2.9 %fusion.3 = bf16[1,2,128,128]{3,0,2,1:T(2,128)(2,1)S(1)} fusion(bf16[32,2,128,128]{3,2,1,0:T(8,128)(2,1)} %bitcast.39, s32[]{:T(128)S(6)} %axis_index.12), kind=kOutput, calls=%fused_computation.4 | convolution fusion | flops 2097184 | bytes 2162692 | tf_op jit(solution)/shard_map/n,nhab->hab/dot_general | solution.py:27
  173.2 0.1 copy.15
  173.3 0.2 multiply_reduce_fusion
  173.5 0.0 copy-done.1
  173.6 0.1 multiply_convert_fusion
  173.7 58.3 %all-gather.7.cloned.1.call-done = bf16[256,4096]{1,0:T(8,128)(2,1)} async-done(((bf16[256,256]{1,0:T(8,128)(2,1)}), bf16[256,4096]{1,0:T(8,128)(2,1)}) %all-gather.7.cloned.1.call-update) | async-done | bytes 2097168 | tf_op jit(solution)/shard_map/all_gather | solution.py:40
  231.9 3.6 %fusion = bf16[1,256,4096]{2,1,0:T(8,128)(2,1)} fusion(bf16[256,256]{0,1:T(8,128)(2,1)S(1)} %bitcast.40, bf16[256,4096]{1,0:T(8,128)(2,1)} %all-gather.7.cloned.1.call-done), kind=kOutput, calls=%fused_computation.1 | convolution fusion | flops 537919488 | bytes 4325376 | tf_op jit(solution)/shard_map/dot_general | solution.py:39
  (3 shorter events, 0.0 us)
Async XLA Ops:
  6.5 85.8 %copy-start = (bf16[1,256,4096]{2,1,0:T(8,128)(2,1)S(1)}, bf16[1,256,4096]{2,1,0:T(8,128)(2,1)}, u32[]{:S(2)}) copy-start(bf16[1,256,4096]{2,1,0:T(8,128)(2,1)} %param.4) | copy-start | bytes 6291460
  6.5 85.8 %all-gather.5.cloned.1.call-start = ((), (), s32[]{:S(2)}) async-start(), calls=%async_computation | async-start | bytes 6684672 | tf_op jit(solution)/shard_map/all_gather | solution.py:16
  7.3 163.1 %all-gather.9.cloned.1.call-start = ((), (), s32[]{:S(2)}) async-start(), calls=%async_computation.2 | async-start | bytes 2162688 | tf_op jit(solution)/shard_map/all_gather | solution.py:22
  98.2 75.4 %copy-start.1 = (f32[256]{0:T(256)S(1)}, f32[256]{0:T(256)}, u32[]{:S(2)}) copy-start(f32[256]{0:T(256)} %param.6) | copy-start | bytes 3076
  98.2 133.7 %all-gather.7.cloned.1.call-start = ((), (), s32[]{:S(2)}) async-start(), calls=%async_computation.1 | async-start | bytes 2228224 | tf_op jit(solution)/shard_map/all_gather | solution.py:40
Sparse Core Ops, SparseCore 0:
  10.4 81.9 all-gather.4
  98.3 71.9 all-gather.8
  173.3 58.5 all-gather.6
where the time goes:
time: 242 us
  waiting for transfers between devices  216 us (89%)
  between operations  13.2 us (5%)
  matrix products  12.4 us (5%)
    all_gather x1, waiting for transfers between devices, shards(): lax.all_gather(w_qkv, 'dp', axis=0, tiled=True)  85.1 us
    all_gather x1, waiting for transfers between devices, shards(): lax.all_gather(state[None].astype(jnp.bfloat16), 'seq', axis=0, tiled=True)  71 us
    all_gather x1, waiting for transfers between devices, shards(): lax.all_gather(w_out, 'dp', axis=1, tiled=True)  58.3 us
  transfers between devices with their start and end apart: 3, of which 3 were waited for; matrix products, arithmetic and copies ran while one was open for 2% of the time, Pallas kernels for 0%

commit v1 on v0

--- a/solution.py
+++ b/solution.py
@@ -19,8 +19,11 @@
     keys = jax.nn.silu(proj[:, feat : 2 * feat]).astype(jnp.bfloat16).reshape(tok_rows, heads, HEAD)
     values = proj[:, 2 * feat :].astype(jnp.bfloat16).reshape(tok_rows, heads, HEAD)
     state = jnp.einsum("thA,thB->hAB", keys, values, preferred_element_type=jnp.float32)
-    every_state = lax.all_gather(
-        state[None].astype(jnp.bfloat16), "seq", axis=0, tiled=True
+    every_state = jnp.concatenate(
+        lax.all_to_all(
+            jnp.stack([state[None].astype(jnp.bfloat16)] * lax.axis_size("seq")), "seq", 0, 0
+        ),
+        axis=0,
     ).astype(jnp.float32)
     blocks = every_state.shape[0]
     weights = (jnp.arange(blocks) < lax.axis_index("seq")).astype(jnp.float32)

time: 242 us -> 225 us (0.930)
  waiting for transfers between devices: 216 us -> 184 us
  starting transfers between devices: 0.08 us -> 13.1 us
    all_to_all x0 -> x1, waiting for transfers between devices: none -> 97.5 us  [shards(): lax.all_to_all(jnp.stack([state[None].astype(jnp.bfloat16)] * lax.axis_si...]
    all_gather x1 -> x0, waiting for transfers between devices: 71 us -> none  [shards(): lax.all_gather(state[None].astype(jnp.bfloat16), 'seq', axis=0, tiled=True)]
    all_gather x1, waiting for transfers between devices: 58.3 us -> 0.02 us  [shards(): lax.all_gather(w_out, 'dp', axis=1, tiled=True)]
    all_to_all x0 -> x1, starting transfers between devices: none -> 13.1 us  [shards(): lax.all_to_all(jnp.stack([state[None].astype(jnp.bfloat16)] * lax.axis_si...]
  transfers between devices with their start and end apart: 3 -> 3, of which waited for: 3 -> 2; matrix products, arithmetic and copies ran while one was open for 2% -> 2% of each run, Pallas kernels for 0% -> 0%
where the time goes in v1:
time: 225 us
  waiting for transfers between devices  184 us (82%)
  between operations  13.5 us (6%)
  starting transfers between devices  13.1 us (6%)
  matrix products  11.8 us (5%)
    all_to_all x1, waiting for transfers between devices, shards(): lax.all_to_all(jnp.stack([state[None].astype(jnp.bfloat16)] * lax.axis_si...  97.5 us
    all_gather x1, waiting for transfers between devices, shards(): lax.all_gather(w_qkv, 'dp', axis=0, tiled=True)  85.1 us
    all_to_all x1, starting transfers between devices, shards(): lax.all_to_all(jnp.stack([state[None].astype(jnp.bfloat16)] * lax.axis_si...  13.1 us
    dot_general x1, matrix products, shards(): jnp.dot(inputs, lax.all_gather(w_qkv, 'dp', axis=0, tiled=True), preferre...  4.56 us
  transfers between devices with their start and end apart: 3, of which 2 were waited for; matrix products, arithmetic and copies ran while one was open for 2% of the time, Pallas kernels for 0%

profile of v1, /device:TPU:1, one launch (start us, length us, event | category | flops | bytes accessed | tf_op | source)
XLA Modules:
  0.0 224.9 jit_solution(2538164592610223415)
XLA Ops:
  6.5 0.0 copy-start
  6.5 0.0 all-gather.3.cloned.1.call-start
  6.5 0.7 all-gather.3.cloned.1.call-update
  7.3 85.1 %all-gather.3.cloned.1.call-done = bf16[4096,768]{1,0:T(8,128)(2,1)} async-done(((bf16[256,768]{1,0:T(8,128)(2,1)}), bf16[4096,768]{1,0:T(8,128)(2,1)}) %all-gather.3.cloned.1.call-update) | async-done | bytes 6291472 | tf_op jit(solution)/shard_map/all_gather | solution.py:16
  92.4 0.0 copy-done
  92.4 4.6 %fusion.1 = f32[256,768]{1,0:T(8,128)S(1)} fusion(bf16[4096,768]{1,0:T(8,128)(2,1)} %all-gather.3.cloned.1.call-done, bf16[1,256,4096]{2,1,0:T(8,128)(2,1)S(1)} %copy-done), kind=kOutput, calls=%fused_computation.2 | convolution fusion | flops 1610612736 | bytes 9175040 | tf_op jit(solution)/shard_map/dot_general | solution.py:15
  96.9 0.1 fusion.13
  97.1 0.1 copy.12
  97.2 0.1 copy.13
  97.3 0.2 convolution_convert_fusion.1
  97.5 1.8 stack.2
  99.4 13.1 %all-to-all-start = ((bf16[32,1,2,128,128]{4,3,2,1,0:T(8,128)(2,1)}), bf16[32,1,2,128,128]{4,3,2,1,0:T(8,128)(2,1)}, u32[]{:S(2)}, u32[]{:S(2)}) async-start(bf16[32,1,2,128,128]{4,3,2,1,0:T(8,128)(2,1)} %stack.2), calls=%async_computation | async-start | bytes 4194304 | tf_op jit(solution)/shard_map/all_to_all | solution.py:23
  112.4 0.0 copy-start.1
  112.4 0.0 all-gather.5.cloned.1.call-start
  112.5 0.7 all-gather.5.cloned.1.call-update
  113.2 0.4 fusion.6
  113.6 97.5 %all-to-all-done = bf16[32,1,2,128,128]{4,3,2,1,0:T(8,128)(2,1)} async-done(((bf16[32,1,2,128,128]{4,3,2,1,0:T(8,128)(2,1)}), bf16[32,1,2,128,128]{4,3,2,1,0:T(8,128)(2,1)}, u32[]{:S(2)}, u32[]{:S(2)}) %all-to-all-start) | async-done | bytes 2097184 | tf_op jit(solution)/shard_map/all_to_all | solution.py:23
  211.1 2.9 %fusion.3 = bf16[1,2,128,128]{3,0,2,1:T(2,128)(2,1)S(1)} fusion(bf16[32,2,128,128]{3,2,1,0:T(8,128)(2,1)} %bitcast.4, s32[]{:T(128)S(6)} %axis_index.12), kind=kOutput, calls=%fused_computation.4 | convolution fusion | flops 2097184 | bytes 2162692 | tf_op jit(solution)/shard_map/n,nhab->hab/dot_general | solution.py:30
  213.9 0.1 copy.11
  214.1 0.2 multiply_reduce_fusion
  214.3 0.0 copy-done.1
  214.3 0.1 multiply_convert_fusion
  214.4 0.0 all-gather.5.cloned.1.call-done
  214.4 3.6 %fusion = bf16[1,256,4096]{2,1,0:T(8,128)(2,1)} fusion(bf16[256,256]{0,1:T(8,128)(2,1)S(1)} %bitcast.39, bf16[256,4096]{1,0:T(8,128)(2,1)} %all-gather.5.cloned.1.call-done), kind=kOutput, calls=%fused_computation.1 | convolution fusion | flops 537919488 | bytes 4325376 | tf_op jit(solution)/shard_map/dot_general | solution.py:42
  (3 shorter events, 0.0 us)
Async XLA Ops:
  6.5 85.8 %copy-start = (bf16[1,256,4096]{2,1,0:T(8,128)(2,1)S(1)}, bf16[1,256,4096]{2,1,0:T(8,128)(2,1)}, u32[]{:S(2)}) copy-start(bf16[1,256,4096]{2,1,0:T(8,128)(2,1)} %param.4) | copy-start | bytes 6291460
  6.5 85.8 %all-gather.3.cloned.1.call-start = ((), (), s32[]{:S(2)}) async-start(), calls=%async_computation.1 | async-start | bytes 6684672 | tf_op jit(solution)/shard_map/all_gather | solution.py:16
  99.4 111.7 %all-to-all-start = ((bf16[32,1,2,128,128]{4,3,2,1,0:T(8,128)(2,1)}), bf16[32,1,2,128,128]{4,3,2,1,0:T(8,128)(2,1)}, u32[]{:S(2)}, u32[]{:S(2)}) async-start(bf16[32,1,2,128,128]{4,3,2,1,0:T(8,128)(2,1)} %stack.2), calls=%async_computation | async-start | bytes 4194304 | tf_op jit(solution)/shard_map/all_to_all | solution.py:23
  112.4 101.8 %copy-start.1 = (f32[256]{0:T(256)S(1)}, f32[256]{0:T(256)}, u32[]{:S(2)}) copy-start(f32[256]{0:T(256)} %param.6) | copy-start | bytes 3076
  112.4 102.0 %all-gather.5.cloned.1.call-start = ((), (), s32[]{:S(2)}) async-start(), calls=%async_computation.2 | async-start | bytes 2228224 | tf_op jit(solution)/shard_map/all_gather | solution.py:43
Sparse Core Ops, SparseCore 0:
  10.4 81.9 all-gather.2
  116.3 61.0 all-gather.4
